TPU v7x, 32 devices: a whole 2x2x4 slice. The times are simulated.
32 devices in a mesh: seq: 16 (over z, x, core), ch: 2 (over y).
Axes of the slice: x: 2, y: 2, z: 4, core: 2. Of those that a mesh axis runs over, the one named last changes fastest.
Arguments:
- tokens: bfloat16 [131072, 1024], P('seq', 'ch'), may hold values from -6 to 6
- right_block: bfloat16 [1024, 1024], P('seq'), may hold values from -0.1875 to 0.1875
- twiddle: bfloat16 [128, 1024], P('seq'), may hold values from -4 to 4
- left_block: bfloat16 [128, 128], replicated, may hold values from -0.5 to 0.5
- gain: float32 [1024], replicated, may hold values from 0.1 to 1.9
- mix_weight: bfloat16 [4, 256, 256], replicated, may hold values from -0.375 to 0.375
Outputs:
- layer_out: bfloat16 [131072, 1024], P(('seq', 'ch'))
All inputs are finite; a program needn't handle non-finite values.
Results may differ from a plain program's by a relative error of at most 0.007.
Values may be sent and summed in bfloat16 or wider, within the bound.
No kernel may reach another device: no remote copies, remote signals or barrier semaphores. Data moves between devices by JAX's collectives and lax.ppermute only.
A program may use at most 128 MiB of HBM per device.

v0:
```python
import jax
import jax.numpy as jnp
from jax import lax
from jax.sharding import PartitionSpec as P


def body(tokens, right_block, twiddle, left_block, gain, mix_weight):
    row_width = right_block.shape[1]
    row_count = tokens.shape[0] // row_width
    local_width = tokens.shape[1]
    inputs = tokens.reshape(row_count, row_width, local_width)
    whole_right = lax.all_gather(right_block, "seq", axis=0, tiled=True)
    first_section = jnp.einsum(
        "abc,bk->akc", inputs, whole_right, preferred_element_type=jnp.float32
    )
    spread = (first_section * twiddle.astype(jnp.float32)[:, :, None]).astype(jnp.bfloat16)
    mixed_rows = jnp.einsum(
        "ij,jbc->ibc",
        left_block,
        lax.all_to_all(spread, "seq", split_axis=1, concat_axis=0, tiled=True),
        preferred_element_type=jnp.float32,
    ).astype(jnp.bfloat16)
    sequence_mixed = lax.all_to_all(mixed_rows, "seq", split_axis=0, concat_axis=1, tiled=True)
    gated = (sequence_mixed.astype(jnp.float32) * jax.nn.silu(inputs.astype(jnp.float32))).astype(
        jnp.bfloat16
    )
    ch_count = lax.axis_size("ch")
    pieces = gated.reshape(ch_count, row_count * row_width // ch_count, local_width)
    shard_piece = lax.all_to_all(pieces, "ch", split_axis=0, concat_axis=2, tiled=True)
    values = shard_piece.astype(jnp.float32)
    inverse_rms = lax.rsqrt(jnp.mean(values * values, axis=-1, keepdims=True) + 1e-05)
    normed = (values * inverse_rms * gain).astype(jnp.bfloat16)
    block_count = mix_weight.shape[0]
    block_width = mix_weight.shape[1]
    normed = normed.reshape(shard_piece.shape[0], shard_piece.shape[1], block_count, block_width)
    result = jnp.einsum("otki,kij->otkj", normed, mix_weight, preferred_element_type=jnp.float32)
    mixed_out = result.astype(jnp.bfloat16).reshape(shard_piece.shape)
    return mixed_out.reshape(mixed_out.shape[1], mixed_out.shape[2])


def solution(mesh):
    in_specs = (P("seq", "ch"), P("seq", None), P("seq", None), P(), P(), P())
    out_specs = P(("seq", "ch"), None)
    return jax.shard_map(body, mesh=mesh, in_specs=in_specs, out_specs=out_specs, check_vma=False)
```

profile of v0, /device:TPU:0, one launch (start us, length us, event | category | flops | bytes accessed | tf_op | source)
XLA Modules:
  0.0 688.4 jit_solution(9891246923339993870)
XLA Ops:
  6.5 0.0 copy-start
  6.5 0.0 all-gather.2.cloned.1.call-start
  6.5 0.7 all-gather.2.cloned.1.call-update
  7.3 0.7 convert_element_type.77
  8.0 45.7 %all-gather.2.cloned.1.call-done = bf16[1024,1024]{1,0:T(8,128)(2,1)} async-done(((bf16[64,1024]{1,0:T(8,128)(2,1)}), bf16[1024,1024]{1,0:T(8,128)(2,1)}) %all-gather.2.cloned.1.call-update) | async-done | bytes 2097168 | tf_op jit(solution)/shard_map/all_gather | solution.py:12
  53.7 14.9 %fusion.5 = bf16[8,1024,512]{2,1,0:T(8,128)(2,1)} fusion(bf16[8,1024,512]{2,1,0:T(8,128)(2,1)} %bitcast.44, f32[8,1024]{1,0:T(8,128)S(1)} %convert_element_type.77, bf16[1024,1024]{1,0:T(8,128)(2,1)} %all-gather.2.cloned.1.call-done), kind=kOutput, calls=%fused_computation.11 | convolution fusion | flops 8598323200 | bytes 18907136 | tf_op jit(solution)/shard_map/abc,bk->akc/dot_general | solution.py:13
  68.6 11.3 %copy.26 = bf16[8,1024,512]{2,0,1:T(8,128)(2,1)} copy(bf16[8,1024,512]{2,1,0:T(8,128)(2,1)} %fusion.5) | data formatting | bytes 16777216 | tf_op jit(solution)/shard_map/convert_element_type | solution.py:16
  79.9 186.7 %all_to_all.36 = bf16[8,1024,512]{2,0,1:T(8,128)(2,1)} all-to-all(bf16[8,1024,512]{2,0,1:T(8,128)(2,1)} %copy.26), channel_id=1, replica_groups=mesh['seq'=16,'ch'=2] {'seq'}, dimensions={1} | all-to-all | bytes 16777216 | tf_op jit(solution)/shard_map/all_to_all | solution.py:20
  266.6 0.0 copy-start.1
  266.6 10.3 %copy.28 = bf16[16,8,64,512]{3,2,1,0:T(8,128)(2,1)} copy(bf16[16,8,64,512]{3,1,2,0:T(8,128)(2,1)} %bitcast.42) | data formatting | bytes 16777216 | tf_op jit(solution)/shard_map/all_to_all | solution.py:20
  276.9 0.0 copy-done.1
  276.9 22.3 %convert_bitcast_fusion.2 = bf16[128,64,512]{0,2,1:T(8,128)(2,1)} fusion(bf16[128,64,512]{2,1,0:T(8,128)(2,1)} %bitcast.43, bf16[128,128]{1,0:T(8,128)(2,1)S(1)} %copy-done.1), kind=kOutput, calls=%fused_computation.19 | convolution fusion | flops 1077936128 | bytes 16809984 | tf_op jit(solution)/shard_map/ij,jbc->ibc/dot_general | solution.py:17
  299.2 12.6 %copy.30 = bf16[128,64,512]{2,1,0:T(8,128)(2,1)} copy(bf16[128,64,512]{0,2,1:T(8,128)(2,1)} %convert_bitcast_fusion.2) | data formatting | bytes 16777216 | tf_op jit(solution)/shard_map/convert_element_type | solution.py:22
  311.9 187.2 %all_to_all.37 = bf16[128,64,512]{2,1,0:T(8,128)(2,1)} all-to-all(bf16[128,64,512]{2,1,0:T(8,128)(2,1)} %copy.30), channel_id=1, replica_groups=mesh['seq'=16,'ch'=2] {'seq'}, dimensions={0} | all-to-all | bytes 16777216 | tf_op jit(solution)/shard_map/all_to_all | solution.py:23
  499.1 0.0 slice-start
  499.1 11.7 %convert_bitcast_fusion.1 = f32[8,16,64,512]{3,2,0,1:T(8,128)} fusion(bf16[16,8,64,512]{3,2,1,0:T(8,128)(2,1)} %bitcast.40), kind=kLoop, calls=%fused_computation.9 | loop fusion | flops 4194304 | bytes 25165824 | tf_op jit(solution)/shard_map/convert_element_type | solution.py:24
  510.8 0.0 slice-start.1
  510.8 7.1 %copy.31 = f32[8,16,64,512]{3,2,1,0:T(8,128)S(1)} copy(f32[8,16,64,512]{3,2,0,1:T(8,128)} %convert_bitcast_fusion.1) | data formatting | bytes 33554432 | tf_op jit(solution)/shard_map/convert_element_type | solution.py:24
  517.9 0.0 slice-done
  518.0 0.0 slice-done.1
  518.0 7.0 %fusion.6 = bf16[2,4096,512]{2,1,0:T(8,128)(2,1)} fusion(f32[2,4096,512]{2,1,0:T(8,128)S(1)} %bitcast.39, bf16[2,4096,512]{2,1,0:T(8,128)(2,1)S(1)} %bitcast.47), kind=kLoop, calls=%fused_computation.13 | loop fusion | flops 29360128 | bytes 33554432 | tf_op jit(solution)/shard_map/convert_element_type | solution.py:24
  525.0 0.0 copy-start.2
  525.0 7.3 %all-to-all-start.2 = ((bf16[2,4096,512]{2,1,0:T(8,128)(2,1)}), bf16[2,4096,512]{2,1,0:T(8,128)(2,1)}, u32[]{:S(2)}, u32[]{:S(2)}) async-start(bf16[2,4096,512]{2,1,0:T(8,128)(2,1)} %fusion.6), calls=%async_computation.2 | async-start | bytes 16777216 | tf_op jit(solution)/shard_map/all_to_all | solution.py:29
  532.3 0.0 copy-done.2
  532.3 93.7 %all-to-all-done.2 = bf16[2,4096,512]{2,1,0:T(8,128)(2,1)} async-done(((bf16[2,4096,512]{2,1,0:T(8,128)(2,1)}), bf16[2,4096,512]{2,1,0:T(8,128)(2,1)}, u32[]{:S(2)}, u32[]{:S(2)}) %all-to-all-start.2) | async-done | bytes 8388640 | tf_op jit(solution)/shard_map/all_to_all | solution.py:29
  626.0 5.1 fusion
  631.1 11.5 %convert_bitcast_fusion = f32[1,4096,2,512]{3,1,2,0:T(8,128)} fusion(bf16[2,4096,512]{2,1,0:T(8,128)(2,1)} %all-to-all-done.2), kind=kLoop, calls=%fused_computation.3 | loop fusion | flops 4194304 | bytes 25165824 | tf_op jit(solution)/shard_map/convert_element_type | solution.py:30
  642.7 17.6 %copy.32 = f32[1,4096,2,512]{1,3,2,0:T(8,128)} copy(f32[1,4096,2,512]{3,1,2,0:T(8,128)} %convert_bitcast_fusion) | data formatting | bytes 33554432 | tf_op jit(solution)/shard_map/convert_element_type | solution.py:30
  660.2 0.0 copy-done
  660.2 9.2 %fusion.12 = bf16[4,4096,256]{1,2,0:T(8,128)(2,1)} fusion(bf16[4,256,256]{2,1,0:T(8,128)(2,1)S(1)} %copy-done, f32[4096,4,256]{0,2,1:T(8,128)} %bitcast.38, f32[4,256]{1,0:T(4,128)S(1)} %mul.58, f32[4096]{0:T(1024)S(1)} %add_rsqrt_fusion), kind=kOutput, calls=%fused_computation.20 | convolution fusion | flops 2164260864 | bytes 25710592 | tf_op jit(solution)/shard_map/otki,kij->otkj/dot_general | solution.py:36
  669.4 11.9 %copy.35 = bf16[4096,1024]{1,0:T(8,128)(2,1)} copy(bf16[4096,1024]{0,1:T(8,128)(2,1)} %bitcast.41) | data formatting | bytes 16777216 | tf_op jit(solution)/shard_map/reshape;reshape | solution.py:38
  (3 shorter events, 0.0 us)
Async XLA Ops:
  6.5 653.7 %copy-start = (bf16[4,256,256]{2,1,0:T(8,128)(2,1)S(1)}, bf16[4,256,256]{2,1,0:T(8,128)(2,1)}, u32[]{:S(2)}) copy-start(bf16[4,256,256]{2,1,0:T(8,128)(2,1)} %param.11) | copy-start | bytes 1572868
  6.5 47.2 %all-gather.2.cloned.1.call-start = ((), (), s32[]{:S(2)}) async-start(), calls=%async_computation.3 | async-start | bytes 2228224 | tf_op jit(solution)/shard_map/all_gather | solution.py:12
  266.6 10.3 %copy-start.1 = (bf16[128,128]{1,0:T(8,128)(2,1)S(1)}, bf16[128,128]{1,0:T(8,128)(2,1)}, u32[]{:S(2)}) copy-start(bf16[128,128]{1,0:T(8,128)(2,1)} %param.9) | copy-start | bytes 98308
  499.1 18.9 %slice-start = ((s8[8388608]{0:T(1024)(128)(4,1)}), s8[4194304]{0:T(1024)(128)(4,1)S(1)}, s32[]{:S(2)}) async-start(s8[8388608]{0:T(1024)(128)(4,1)} %bitcast.45), calls=%async_computation.4 | async-start | bytes 8388608
  510.8 7.1 %slice-start.1 = ((s8[8388608]{0:T(1024)(128)(4,1)}), s8[4194304]{0:T(1024)(128)(4,1)S(1)}, s32[]{:S(2)}) async-start(s8[8388608]{0:T(1024)(128)(4,1)} %bitcast.45), calls=%async_computation.5 | async-start | bytes 8388608
  525.0 7.3 %copy-start.2 = (f32[1024]{0:T(1024)S(1)}, f32[1024]{0:T(1024)}, u32[]{:S(2)}) copy-start(f32[1024]{0:T(1024)} %param.10) | copy-start | bytes 12292
  525.0 101.0 %all-to-all-start.2 = ((bf16[2,4096,512]{2,1,0:T(8,128)(2,1)}), bf16[2,4096,512]{2,1,0:T(8,128)(2,1)}, u32[]{:S(2)}, u32[]{:S(2)}) async-start(bf16[2,4096,512]{2,1,0:T(8,128)(2,1)} %fusion.6), calls=%async_computation.2 | async-start | bytes 16777216 | tf_op jit(solution)/shard_map/all_to_all | solution.py:29
Sparse Core Ops, SparseCore 0:
  9.5 44.1 all-gather.1
where the time goes:
time: 697 us; the launch traced here: 688 us
  blocking collectives  374 us (54%)
  waiting for transfers between devices  140 us (20%)
  local copies, waits for them, and re-layouts  70.9 us (10%)
  matrix products  46.4 us (7%)
  other arithmetic  36.1 us (5%)
  between operations  13.7 us (2%)
  starting transfers between devices  7.29 us (1%)
    all_to_all x1, blocking collectives, body(): lax.all_to_all(mixed_rows, 'seq', split_axis=0, concat_axis=1, tiled=True)  187 us
    all_to_all x1, blocking collectives, body(): lax.all_to_all(spread, 'seq', split_axis=1, concat_axis=0, tiled=True)  187 us
    all_to_all x1, waiting for transfers between devices, body(): lax.all_to_all(pieces, 'ch', split_axis=0, concat_axis=2, tiled=True)  93.7 us
    all_gather x1, waiting for transfers between devices, body(): whole_right = lax.all_gather(right_block, 'seq', axis=0, tiled=True)  45.7 us
    dot_general x1, matrix products, body(): jnp.einsum('ij,jbc->ibc', left_block, lax.all_to_all(spread, 'seq', split...  22.3 us
    convert_element_type x1, local copies, waits for them, and re-layouts, body(): values = shard_piece.astype(jnp.float32)  17.6 us
    dot_general x1, matrix products, body(): jnp.einsum('abc,bk->akc', inputs, whole_right, preferred_element_type=jnp...  14.9 us
  transfers between devices with their start and end apart: 2, of which 2 were waited for; matrix products, arithmetic and copies ran while one was open for 0% of the time, Pallas kernels for 0%

commit v1 on v0

--- a/solution.py
+++ b/solution.py
@@ -17,7 +17,10 @@
     mixed_rows = jnp.einsum(
         "ij,jbc->ibc",
         left_block,
-        lax.all_to_all(spread, "seq", split_axis=1, concat_axis=0, tiled=True),
+        jnp.concatenate(
+            lax.all_to_all(jnp.stack(jnp.split(spread, lax.axis_size("seq"), axis=1)), "seq", 0, 0),
+            axis=0,
+        ),
         preferred_element_type=jnp.float32,
     ).astype(jnp.bfloat16)
     sequence_mixed = lax.all_to_all(mixed_rows, "seq", split_axis=0, concat_axis=1, tiled=True)

time: 697 us -> 661 us (0.948); the launches traced: 688 us -> 660 us
  local copies, waits for them, and re-layouts: 70.9 us -> 49.9 us
    convert_element_type x2 -> x1, local copies, waits for them, and re-layouts: 24 us -> 12.5 us  [body(): mixed_rows = jnp.einsum('ij,jbc->ibc', left_block, jnp.concatenate(lax.al...]
    all_to_all x1 -> x0, local copies, waits for them, and re-layouts: 10.3 us -> none  [body(): lax.all_to_all(spread, 'seq', split_axis=1, concat_axis=0, tiled=True)]
where the time goes in v1:
time: 661 us; the launch traced here: 660 us
  blocking collectives  373 us (56%)
  waiting for transfers between devices  140 us (21%)
  local copies, waits for them, and re-layouts  49.9 us (8%)
  matrix products  39.7 us (6%)
  other arithmetic  36.1 us (5%)
  between operations  13.6 us (2%)
  starting transfers between devices  7.29 us (1%)
    all_to_all x1, blocking collectives, body(): lax.all_to_all(mixed_rows, 'seq', split_axis=0, concat_axis=1, tiled=True)  188 us
    all_to_all x1, blocking collectives, body(): lax.all_to_all(jnp.stack(jnp.split(spread, lax.axis_size('seq'), axis=1))...  185 us
    all_to_all x1, waiting for transfers between devices, body(): lax.all_to_all(pieces, 'ch', split_axis=0, concat_axis=2, tiled=True)  93.7 us
    all_gather x1, waiting for transfers between devices, body(): whole_right = lax.all_gather(right_block, 'seq', axis=0, tiled=True)  45.7 us
    dot_general x1, matrix products, body(): jnp.einsum('ij,jbc->ibc', left_block, jnp.concatenate(lax.all_to_all(jnp....  17.6 us
    convert_element_type x1, local copies, waits for them, and re-layouts, body(): values = shard_piece.astype(jnp.float32)  17.6 us
  transfers between devices with their start and end apart: 2, of which 2 were waited for; matrix products, arithmetic and copies ran while one was open for 0% of the time, Pallas kernels for 0%

profile of v1, /device:TPU:0, one launch (start us, length us, event | category | flops | bytes accessed | tf_op | source)
XLA Modules:
  0.0 659.7 jit_solution(13335346247552084549)
XLA Ops:
  6.5 0.0 copy-start
  6.5 0.0 all-gather.2.cloned.1.call-start
  6.5 0.7 all-gather.2.cloned.1.call-update
  7.3 0.7 convert_element_type.77
  8.0 45.7 %all-gather.2.cloned.1.call-done = bf16[1024,1024]{1,0:T(8,128)(2,1)} async-done(((bf16[64,1024]{1,0:T(8,128)(2,1)}), bf16[1024,1024]{1,0:T(8,128)(2,1)}) %all-gather.2.cloned.1.call-update) | async-done | bytes 2097168 | tf_op jit(solution)/shard_map/all_gather | solution.py:12
  53.7 12.9 %fusion.5 = bf16[8,1024,512]{2,1,0:T(8,128)(2,1)S(1)} fusion(bf16[8,1024,512]{2,1,0:T(8,128)(2,1)} %bitcast.104, f32[8,1024]{1,0:T(8,128)S(1)} %convert_element_type.77, bf16[1024,1024]{1,0:T(8,128)(2,1)} %all-gather.2.cloned.1.call-done), kind=kOutput, calls=%fused_computation.11 | convolution fusion | flops 8598323200 | bytes 18907136 | tf_op jit(solution)/shard_map/abc,bk->akc/dot_general | solution.py:13
  67.4 0.0 copy-start.1
  67.4 185.2 %all_to_all.23 = bf16[16,8,64,512]{3,2,1,0:T(8,128)(2,1)S(1)} all-to-all(bf16[16,8,64,512]{3,2,1,0:T(8,128)(2,1)S(1)} %fusion.16), channel_id=1, replica_groups=mesh['seq'=16,'ch'=2] {'seq'}, dimensions={0} | all-to-all | bytes 16777216 | tf_op jit(solution)/shard_map/all_to_all | solution.py:21
  252.7 0.0 copy-done.1
  252.7 17.6 %convert_bitcast_fusion.2 = bf16[128,64,512]{0,2,1:T(8,128)(2,1)} fusion(bf16[128,64,512]{2,1,0:T(8,128)(2,1)S(1)} %bitcast.103, bf16[128,128]{1,0:T(8,128)(2,1)S(1)} %copy-done.1), kind=kOutput, calls=%fused_computation.19 | convolution fusion | flops 1077936128 | bytes 16809984 | tf_op jit(solution)/shard_map/ij,jbc->ibc/dot_general | solution.py:17
  270.3 12.5 %copy.18 = bf16[128,64,512]{2,1,0:T(8,128)(2,1)} copy(bf16[128,64,512]{0,2,1:T(8,128)(2,1)} %convert_bitcast_fusion.2) | data formatting | bytes 16777216 | tf_op jit(solution)/shard_map/convert_element_type | solution.py:25
  282.8 187.8 %all_to_all.24 = bf16[128,64,512]{2,1,0:T(8,128)(2,1)} all-to-all(bf16[128,64,512]{2,1,0:T(8,128)(2,1)} %copy.18), channel_id=1, replica_groups=mesh['seq'=16,'ch'=2] {'seq'}, dimensions={0} | all-to-all | bytes 16777216 | tf_op jit(solution)/shard_map/all_to_all | solution.py:26
  470.6 0.0 slice-start
  470.6 11.7 %convert_bitcast_fusion.1 = f32[8,16,64,512]{3,2,0,1:T(8,128)} fusion(bf16[16,8,64,512]{3,2,1,0:T(8,128)(2,1)} %bitcast.101), kind=kLoop, calls=%fused_computation.9 | loop fusion | flops 4194304 | bytes 25165824 | tf_op jit(solution)/shard_map/convert_element_type | solution.py:27
  482.3 0.0 slice-start.1
  482.3 7.1 %copy.19 = f32[8,16,64,512]{3,2,1,0:T(8,128)S(1)} copy(f32[8,16,64,512]{3,2,0,1:T(8,128)} %convert_bitcast_fusion.1) | data formatting | bytes 33554432 | tf_op jit(solution)/shard_map/convert_element_type | solution.py:27
  489.4 0.0 slice-done
  489.4 0.0 slice-done.1
  489.5 7.0 %fusion.6 = bf16[2,4096,512]{2,1,0:T(8,128)(2,1)} fusion(f32[2,4096,512]{2,1,0:T(8,128)S(1)} %bitcast.100, bf16[2,4096,512]{2,1,0:T(8,128)(2,1)S(1)} %bitcast.107), kind=kLoop, calls=%fused_computation.13 | loop fusion | flops 29360128 | bytes 33554432 | tf_op jit(solution)/shard_map/convert_element_type | solution.py:27
  496.5 0.0 copy-start.2
  496.5 7.3 %all-to-all-start.2 = ((bf16[2,4096,512]{2,1,0:T(8,128)(2,1)}), bf16[2,4096,512]{2,1,0:T(8,128)(2,1)}, u32[]{:S(2)}, u32[]{:S(2)}) async-start(bf16[2,4096,512]{2,1,0:T(8,128)(2,1)} %fusion.6), calls=%async_computation.2 | async-start | bytes 16777216 | tf_op jit(solution)/shard_map/all_to_all | solution.py:32
  503.8 0.0 copy-done.2
  503.8 93.7 %all-to-all-done.2 = bf16[2,4096,512]{2,1,0:T(8,128)(2,1)} async-done(((bf16[2,4096,512]{2,1,0:T(8,128)(2,1)}), bf16[2,4096,512]{2,1,0:T(8,128)(2,1)}, u32[]{:S(2)}, u32[]{:S(2)}) %all-to-all-start.2) | async-done | bytes 8388640 | tf_op jit(solution)/shard_map/all_to_all | solution.py:32
  597.5 5.1 fusion
  602.6 11.5 %convert_bitcast_fusion = f32[1,4096,2,512]{3,1,2,0:T(8,128)} fusion(bf16[2,4096,512]{2,1,0:T(8,128)(2,1)} %all-to-all-done.2), kind=kLoop, calls=%fused_computation.3 | loop fusion | flops 4194304 | bytes 25165824 | tf_op jit(solution)/shard_map/convert_element_type | solution.py:33
  614.2 17.6 %copy.20 = f32[1,4096,2,512]{1,3,2,0:T(8,128)} copy(f32[1,4096,2,512]{3,1,2,0:T(8,128)} %convert_bitcast_fusion) | data formatting | bytes 33554432 | tf_op jit(solution)/shard_map/convert_element_type | solution.py:33
  631.7 0.0 copy-done
  631.7 9.2 %fusion.12 = bf16[4,4096,256]{1,2,0:T(8,128)(2,1)} fusion(bf16[4,256,256]{2,1,0:T(8,128)(2,1)S(1)} %copy-done, f32[4096,4,256]{0,2,1:T(8,128)} %bitcast.99, f32[4,256]{1,0:T(4,128)S(1)} %mul.58, f32[4096]{0:T(1024)S(1)} %add_rsqrt_fusion), kind=kOutput, calls=%fused_computation.20 | convolution fusion | flops 2164260864 | bytes 25710592 | tf_op jit(solution)/shard_map/otki,kij->otkj/dot_general | solution.py:39
  640.9 11.9 %copy.23 = bf16[4096,1024]{1,0:T(8,128)(2,1)} copy(bf16[4096,1024]{0,1:T(8,128)(2,1)} %bitcast.102) | data formatting | bytes 16777216 | tf_op jit(solution)/shard_map/reshape;reshape | solution.py:41
  (19 shorter events, 0.8 us)
Async XLA Ops:
  6.5 625.2 %copy-start = (bf16[4,256,256]{2,1,0:T(8,128)(2,1)S(1)}, bf16[4,256,256]{2,1,0:T(8,128)(2,1)}, u32[]{:S(2)}) copy-start(bf16[4,256,256]{2,1,0:T(8,128)(2,1)} %param.11) | copy-start | bytes 1572868
  6.5 47.2 %all-gather.2.cloned.1.call-start = ((), (), s32[]{:S(2)}) async-start(), calls=%async_computation.3 | async-start | bytes 2228224 | tf_op jit(solution)/shard_map/all_gather | solution.py:12
  67.4 185.2 %copy-start.1 = (bf16[128,128]{1,0:T(8,128)(2,1)S(1)}, bf16[128,128]{1,0:T(8,128)(2,1)}, u32[]{:S(2)}) copy-start(bf16[128,128]{1,0:T(8,128)(2,1)} %param.9) | copy-start | bytes 98308
  470.6 18.9 %slice-start = ((s8[8388608]{0:T(1024)(128)(4,1)}), s8[4194304]{0:T(1024)(128)(4,1)S(1)}, s32[]{:S(2)}) async-start(s8[8388608]{0:T(1024)(128)(4,1)} %bitcast.105), calls=%async_computation.4 | async-start | bytes 8388608
  482.3 7.1 %slice-start.1 = ((s8[8388608]{0:T(1024)(128)(4,1)}), s8[4194304]{0:T(1024)(128)(4,1)S(1)}, s32[]{:S(2)}) async-start(s8[8388608]{0:T(1024)(128)(4,1)} %bitcast.105), calls=%async_computation.5 | async-start | bytes 8388608
  496.5 7.3 %copy-start.2 = (f32[1024]{0:T(1024)S(1)}, f32[1024]{0:T(1024)}, u32[]{:S(2)}) copy-start(f32[1024]{0:T(1024)} %param.10) | copy-start | bytes 12292
  496.5 101.0 %all-to-all-start.2 = ((bf16[2,4096,512]{2,1,0:T(8,128)(2,1)}), bf16[2,4096,512]{2,1,0:T(8,128)(2,1)}, u32[]{:S(2)}, u32[]{:S(2)}) async-start(bf16[2,4096,512]{2,1,0:T(8,128)(2,1)} %fusion.6), calls=%async_computation.2 | async-start | bytes 16777216 | tf_op jit(solution)/shard_map/all_to_all | solution.py:32
Sparse Core Ops, SparseCore 0:
  9.5 44.1 all-gather.1
